TPU v7x, 256 devices: a whole 4x4x8 slice. The times are simulated.
256 devices in a mesh: front: 8 (over z), row: 4 (over x_hi, core), col: 8 (over x_lo, y).
Axes of the slice: x: 4 (x_hi: 2, x_lo: 2; x = x_hi * 2 + x_lo), y: 4, z: 8, core: 2. Of those that a mesh axis runs over, the one named last changes fastest.
Arguments:
- front_slab: bfloat16 [8, 2048, 8192], P('front', 'row', 'col'), may hold values from -0.0625 to 0.0625
- samples: bfloat16 [8192, 256], P(('row', 'col')), may hold values from -6 to 6
- child_tiles: bfloat16 [512, 128, 2048], P(('front', 'row', 'col')), may hold values from -0.0625 to 0.0625
- parent_front: int32 [512, 1], P(('front', 'row', 'col')), may hold values from 0 to 7; in each aligned block of 2 rows (0 to 1, 2 to 3, ...) at most 2 rows name the same one
- parent_tile: int32 [512], P(('front', 'row', 'col')), may hold values from 0 to 15
- column_tiles: int32 [512, 16], P(('front', 'row', 'col')), may hold values from 0 to 63
- ranks: int32 [8, 4], P('front', 'row'), may hold values from 128 to 256
Outputs:
- sampled: float32 [8, 2048, 256], P('front', ('row', 'col'))
- bases: float32 [8, 2048, 256], P('front', ('row', 'col'))
Inputs may be any that keep to these rules, and one draw needn't show every extreme that they name: `parent_front`: among the 2 tiles of one device, at most 2 name the same parent front.
All inputs are finite; a program needn't handle non-finite values.
Results may differ from a plain program's by a relative error of at most 0.0003.
Values may be sent and summed in bfloat16 or wider, within the bound.
No kernel may reach another device: no remote copies, remote signals or barrier semaphores. Data moves between devices by JAX's collectives and lax.ppermute only.
A program may use at most 64 MiB of HBM per device.

v0:
```python
import math
import jax
import jax.numpy as jnp
from jax import lax
from jax.sharding import PartitionSpec as P


def in_blocks(x, dim, devices):
    before, after = (x.shape[:dim], x.shape[dim + 1 :])
    return jnp.moveaxis(x.reshape(*before, devices, -1, *after), dim, 0)


def summed_on_arrival(x, axis, dim):
    devices = lax.axis_size(axis)
    pieces = lax.all_to_all(in_blocks(x, dim, devices), axis, 0, 0, tiled=True)
    return jnp.sum(pieces, axis=0)


def in_one_piece(arrays, axis, split_dim, concat_dim, along):
    widths = [math.prod(a.shape[along:]) for a in arrays]
    both = jnp.concatenate(
        [a.reshape(*a.shape[:along], w) for a, w in zip(arrays, widths)], axis=along
    )
    out = lax.all_to_all(both, axis, split_axis=split_dim, concat_axis=concat_dim, tiled=True)
    pieces = jnp.split(out, [sum(widths[:k]) for k in range(1, len(widths))], axis=along)
    return tuple((b.reshape(*out.shape[:along], *a.shape[along:]) for a, b in zip(arrays, pieces)))


def sent_to_all(x, axis):
    copies = jnp.broadcast_to(x, (lax.axis_size(axis), *x.shape))
    return lax.all_to_all(copies, axis, split_axis=0, concat_axis=0, tiled=True)


def taken_together(x, axis):
    everything = sent_to_all(x, axis)
    return jnp.sum(everything, axis=0)


def on_device(front_slab, samples, child_tiles, parent_front, parent_tile, column_tiles, ranks):
    width = samples.shape[1]
    slab = front_slab[0]
    col_width = slab.shape[1]
    omega = lax.all_gather(samples, ("row", "col"), axis=0, tiled=True)
    full = omega.shape[0]
    own = lax.dynamic_slice_in_dim(omega, lax.axis_index("col") * col_width, col_width, 0)
    direct = summed_on_arrival(jnp.dot(slab, own, preferred_element_type=jnp.float32), "col", 0)
    tile_count = child_tiles.shape[0]
    blocks = child_tiles.shape[2] // 128
    omega_tiles = omega.reshape(full // 128, 128, width)
    chosen = omega_tiles[column_tiles]
    pieces = child_tiles.reshape(tile_count, 128, blocks, 128)
    product = jnp.einsum("trkc,tkcs->trs", pieces, chosen, preferred_element_type=jnp.float32)
    parents = lax.axis_size("front")
    row_tiles = slab.shape[0] * lax.axis_size("row") // 128
    dest = parent_front[:, 0]
    capacity = max(2, 2 * ((tile_count + parents - 1) // parents))
    match = (dest[:, None] == jnp.arange(parents, dtype=jnp.int32)[None, :]).astype(jnp.int32)
    before = jnp.cumsum(match, axis=0) - match
    slot = dest * capacity + jnp.sum(before * match, axis=1)
    place = (slot[:, None] == jnp.arange(parents * capacity, dtype=jnp.int32)[None, :]).astype(
        jnp.float32
    )
    sent = jnp.einsum("tq,trs->qrs", place, product, precision=lax.Precision.HIGHEST)
    sent = sent.reshape(parents, capacity, 128, width)
    labels = (
        jnp.dot(parent_tile.astype(jnp.float32) + 1.0, place, precision=lax.Precision.HIGHEST) - 1.0
    )
    labels = labels.reshape(parents, capacity)
    arrived, arrived_labels = in_one_piece((sent, labels), "front", 0, 0, 2)
    tile_index = arrived_labels.reshape(-1).astype(jnp.int32)
    spread = (tile_index[:, None] == jnp.arange(row_tiles, dtype=jnp.int32)[None, :]).astype(
        jnp.float32
    )
    gathered = arrived.reshape(parents * capacity, 128, width)
    rows_full = jnp.einsum("qj,qrs->jrs", spread, gathered, precision=lax.Precision.HIGHEST)
    rows_full = rows_full.reshape(row_tiles * 128, width)
    extended = summed_on_arrival(rows_full, ("row", "col"), 0)
    sampled = direct + extended
    mask = (jnp.arange(width, dtype=jnp.int32) < ranks[0, 0]).astype(jnp.float32)
    masked = sampled * mask[None, :]
    partial_gram = jnp.dot(masked.T, masked, precision=lax.Precision.HIGHEST)
    gram = taken_together(partial_gram, "col") + jnp.diag(1.0 - mask)
    lower = jnp.linalg.cholesky(gram)
    basis = lax.linalg.triangular_solve(
        lower, masked, left_side=False, lower=True, transpose_a=True
    )
    return (sampled[None], basis[None])


def solution(mesh):
    in_specs = (
        P("front", "row", "col"),
        P(("row", "col"), None),
        P(("front", "row", "col"), None, None),
        P(("front", "row", "col"), None),
        P(("front", "row", "col")),
        P(("front", "row", "col"), None),
        P("front", "row"),
    )
    out_specs = (P("front", ("row", "col"), None), P("front", ("row", "col"), None))
    return jax.shard_map(
        on_device, mesh=mesh, in_specs=in_specs, out_specs=out_specs, check_vma=False
    )
```

profile of v0, /device:TPU:1, one launch (start us, length us, event | category | flops | bytes accessed | tf_op | source)
XLA Modules:
  0.0 331.1 jit_solution(624082861867423095)
XLA Ops:
  7.2 0.7 all-gather.2.cloned.1.call-update
  7.9 0.7 fusion.22
  8.7 0.8 select_reduce_fusion.2
  9.5 0.7 fusion.23
  10.2 0.8 fusion.2
  11.1 0.7 compare_select_fusion
  11.9 90.9 %all-gather.2.cloned.1.call-done = bf16[8192,256]{1,0:T(8,128)(2,1)} async-done(((bf16[256,256]{1,0:T(8,128)(2,1)}), bf16[8192,256]{1,0:T(8,128)(2,1)}) %all-gather.2.cloned.1.call-update) | async-done | bytes 4194320 | tf_op jit(solution)/shard_map/all_gather | solution.py:43
  102.8 2.9 gather_fusion
  105.7 2.1 convolution_bitcast_fusion.1
  107.8 0.2 copy.19
  108.0 1.2 fusion.20
  109.1 2.5 copy.20
  111.7 2.7 reshape_reshape.13
  114.3 2.3 pad_maximum_fusion
  116.7 7.5 %all-to-all-start.1 = ((f32[8,2,32769]{2,1,0:T(2,128)}), f32[8,2,32769]{2,1,0:T(2,128)S(1)}, u32[]{:S(2)}, u32[]{:S(2)}) async-start(f32[8,2,32769]{2,1,0:T(2,128)} %pad_maximum_fusion), calls=%async_computation.1 | async-start | bytes 4210688 | tf_op jit(solution)/shard_map/all_to_all | solution.py:24
  124.2 2.3 convolution_bitcast_fusion
  126.5 2.0 copy.16
  128.6 47.6 %all-to-all-done.1 = f32[8,2,32769]{2,1,0:T(2,128)S(1)} async-done(((f32[8,2,32769]{2,1,0:T(2,128)}), f32[8,2,32769]{2,1,0:T(2,128)S(1)}, u32[]{:S(2)}, u32[]{:S(2)}) %all-to-all-start.1) | async-done | bytes 2097248 | tf_op jit(solution)/shard_map/all_to_all | solution.py:24
  176.2 4.2 %all-to-all-start = ((f32[8,64,256]{2,1,0:T(8,128)}), f32[8,64,256]{2,1,0:T(8,128)}, u32[]{:S(2)}, u32[]{:S(2)}) async-start(f32[8,64,256]{2,1,0:T(8,128)} %bitcast.87), calls=%async_computation | async-start | bytes 1048576 | tf_op jit(solution)/shard_map/all_to_all | solution.py:15
  180.3 1.5 split.9
  181.8 4.0 %reshape_reshape.15 = f32[16,128,256]{2,1,0:T(8,128)} reshape(f32[8,2,32768]{2,1,0:T(2,128)} %split.9) | data formatting | bytes 4194304 | tf_op jit(solution)/shard_map/reshape;reshape | solution.py:74
  185.8 0.2 fusion.16
  186.1 3.8 %fusion = f32[16,128,256]{2,0,1:T(8,128)S(1)} fusion(f32[16,128,256]{2,1,0:T(8,128)} %reshape_reshape.15, s32[16]{0:T(128)S(1)} %convert_element_type.32), kind=kOutput, calls=%fused_computation.4 | convolution fusion | flops 100663552 | bytes 4194368 | tf_op jit(solution)/shard_map/qj,qrs->jrs/dot_general | solution.py:75
  189.9 2.6 copy.23
  192.5 8.3 %all-to-all-start.2 = ((f32[32,64,256]{2,1,0:T(8,128)}), f32[32,64,256]{2,1,0:T(8,128)S(1)}, u32[]{:S(2)}, u32[]{:S(2)}) async-start(f32[32,64,256]{2,1,0:T(8,128)} %bitcast.15), calls=%async_computation.2 | async-start | bytes 4194304 | tf_op jit(solution)/shard_map/all_to_all | solution.py:15
  201.4 1.1 reduce_sum.40
  202.5 25.7 %all-to-all-done.2 = f32[32,64,256]{2,1,0:T(8,128)S(1)} async-done(((f32[32,64,256]{2,1,0:T(8,128)}), f32[32,64,256]{2,1,0:T(8,128)S(1)}, u32[]{:S(2)}, u32[]{:S(2)}) %all-to-all-start.2) | async-done | bytes 2097184 | tf_op jit(solution)/shard_map/all_to_all | solution.py:15
  228.3 0.6 broadcast_multiply_fusion
  229.0 0.4 fusion.31
  229.4 1.5 broadcast_in_dim.39
  230.9 3.8 %all-to-all-start.3 = ((f32[8,256,256]{2,1,0:T(8,128)}), f32[8,256,256]{2,1,0:T(8,128)S(1)}, u32[]{:S(2)}, u32[]{:S(2)}) async-start(f32[8,256,256]{2,1,0:T(8,128)} %broadcast_in_dim.39), calls=%async_computation.3 | async-start | bytes 4194304 | tf_op jit(solution)/shard_map/all_to_all | solution.py:31
  234.7 26.1 %all-to-all-done.3 = f32[8,256,256]{2,1,0:T(8,128)S(1)} async-done(((f32[8,256,256]{2,1,0:T(8,128)}), f32[8,256,256]{2,1,0:T(8,128)S(1)}, u32[]{:S(2)}, u32[]{:S(2)}) %all-to-all-start.3) | async-done | bytes 2097184 | tf_op jit(solution)/shard_map/all_to_all | solution.py:31
  261.2 11.7 %cholesky.49 = f32[128,128]{1,0:T(8,128)S(1)} custom-call(f32[128,128]{1,0:T(8,128)S(1)} %cholesky.115), custom_call_target="Cholesky" | custom-call | tf_op jit(solution)/shard_map/jit(cholesky)/cholesky | solution.py:83
  273.0 9.8 %custom-call.14 = f32[1,128,128]{1,2,0:T(8,128)S(1)} custom-call(f32[1,128,128]{2,1,0:T(8,128)S(1)} %get-tuple-element.25), custom_call_target="InvertDiagBlocksLowerTriangular" | custom-call | tf_op jit(solution)/shard_map/jit(cholesky)/cholesky | solution.py:83
  282.8 0.2 constant_dynamic-update-slice_fusion.1
  283.0 0.3 convolution_subtract_fusion
  283.3 11.7 %cholesky.103 = f32[128,128]{1,0:T(8,128)S(1)} custom-call(f32[128,128]{1,0:T(8,128)S(1)} %convolution_subtract_fusion), custom_call_target="Cholesky" | custom-call | tf_op jit(solution)/shard_map/jit(cholesky)/cholesky | solution.py:83
  295.1 0.7 compare_reduce_fusion
  297.2 5.3 %while.1 = (s32[]{:T(128)}, f32[256,256]{1,0:T(8,128)S(1)}, s32[2,2]{1,0:T(2,128)S(1)}, f32[2,128,128]{2,1,0:T(8,128)}, s32[]{:T(128)}) while((s32[]{:T(128)}, f32[256,256]{1,0:T(8,128)S(1)}, s32[2,2]{1,0:T(2,128)S(1)}, f32[2,128,128]{2,1,0:T(8,128)}, s32[]{:T(128)}) %tuple.28), condition=%wide.while_cond, body=%wide.while_body.sunk | while | flops 2 | bytes 132205 | solution.py:84
  297.2 0.6 fusion.42
  297.8 2.0 bitcast_dynamic-update-slice_fusion.2
  299.9 0.6 fusion.42
  300.4 2.0 bitcast_dynamic-update-slice_fusion.2
  302.5 20.5 %custom-call.15 = f32[2,128,128]{1,2,0:T(8,128)S(1)} custom-call(f32[2,128,128]{2,1,0:T(8,128)} %get-tuple-element.9), custom_call_target="InvertDiagBlocksLowerTriangular" | custom-call | tf_op jit(solution)/shard_map/triangular_solve | solution.py:84
  323.0 0.2 fusion.11
  323.2 0.2 convolution_subtract_fusion.1
  323.4 0.2 fusion.9
  323.6 0.6 maximum_bitcast_fusion
  (25 shorter events, 1.1 us)
Async XLA Ops:
  7.2 117.0 %copy-start = (bf16[1,512,1024]{2,1,0:T(8,128)(2,1)S(1)}, bf16[1,512,1024]{2,1,0:T(8,128)(2,1)}, u32[]{:S(2)}) copy-start(bf16[1,512,1024]{2,1,0:T(8,128)(2,1)} %param.7) | copy-start | bytes 3145732
  7.2 95.6 %all-gather.2.cloned.1.call-start = ((), (), s32[]{:S(2)}) async-start(), calls=%async_computation.4 | async-start | bytes 4325376 | tf_op jit(solution)/shard_map/all_gather | solution.py:43
  116.7 59.5 %all-to-all-start.1 = ((f32[8,2,32769]{2,1,0:T(2,128)}), f32[8,2,32769]{2,1,0:T(2,128)S(1)}, u32[]{:S(2)}, u32[]{:S(2)}) async-start(f32[8,2,32769]{2,1,0:T(2,128)} %pad_maximum_fusion), calls=%async_computation.1 | async-start | bytes 4210688 | tf_op jit(solution)/shard_map/all_to_all | solution.py:24
  176.2 16.3 %all-to-all-start = ((f32[8,64,256]{2,1,0:T(8,128)}), f32[8,64,256]{2,1,0:T(8,128)}, u32[]{:S(2)}, u32[]{:S(2)}) async-start(f32[8,64,256]{2,1,0:T(8,128)} %bitcast.87), calls=%async_computation | async-start | bytes 1048576 | tf_op jit(solution)/shard_map/all_to_all | solution.py:15
  192.5 35.7 %all-to-all-start.2 = ((f32[32,64,256]{2,1,0:T(8,128)}), f32[32,64,256]{2,1,0:T(8,128)S(1)}, u32[]{:S(2)}, u32[]{:S(2)}) async-start(f32[32,64,256]{2,1,0:T(8,128)} %bitcast.15), calls=%async_computation.2 | async-start | bytes 4194304 | tf_op jit(solution)/shard_map/all_to_all | solution.py:15
  230.9 29.9 %all-to-all-start.3 = ((f32[8,256,256]{2,1,0:T(8,128)}), f32[8,256,256]{2,1,0:T(8,128)S(1)}, u32[]{:S(2)}, u32[]{:S(2)}) async-start(f32[8,256,256]{2,1,0:T(8,128)} %broadcast_in_dim.39), calls=%async_computation.3 | async-start | bytes 4194304 | tf_op jit(solution)/shard_map/all_to_all | solution.py:31
Sparse Core Ops, SparseCore 0:
  9.8 92.9 all-gather.1
where the time goes:
time: 332 us; the launch traced here: 331 us
  waiting for transfers between devices  191 us (58%)
  other arithmetic  62.8 us (19%)
  local copies, waits for them, and re-layouts  25.6 us (8%)
  starting transfers between devices  23.8 us (7%)
  between operations  16.2 us (5%)
  matrix products  11.7 us (4%)
    all_gather x1, waiting for transfers between devices, on_device(): omega = lax.all_gather(samples, ('row', 'col'), axis=0, tiled=True)  90.9 us
    all_to_all x1, waiting for transfers between devices, in_one_piece(): lax.all_to_all(both, axis, split_axis=split_dim, concat_axis=concat_dim,...  47.6 us
    another operation x6, other arithmetic, on_device(): lower = jnp.linalg.cholesky(gram)  34 us
    all_to_all x1, waiting for transfers between devices, sent_to_all(): return lax.all_to_all(copies, axis, split_axis=0, concat_axis=0, tiled=True)  26.1 us
    all_to_all x2, waiting for transfers between devices, summed_on_arrival(): pieces = lax.all_to_all(in_blocks(x, dim, devices), axis, 0, 0, tiled=True)  25.7 us
    another operation x3, other arithmetic, on_device(): lax.linalg.triangular_solve(lower, masked, left_side=False, lower=True, t...  20.5 us
    all_to_all x2, starting transfers between devices, summed_on_arrival(): pieces = lax.all_to_all(in_blocks(x, dim, devices), axis, 0, 0, tiled=True)  12.4 us
    all_to_all x1, starting transfers between devices, in_one_piece(): lax.all_to_all(both, axis, split_axis=split_dim, concat_axis=concat_dim,...  7.52 us
  transfers between devices with their start and end apart: 5, of which 4 were waited for; matrix products, arithmetic and copies ran while one was open for 7% of the time, Pallas kernels for 0%

commit v1 on v0

--- a/solution.py
+++ b/solution.py
@@ -40,7 +40,10 @@
     width = samples.shape[1]
     slab = front_slab[0]
     col_width = slab.shape[1]
-    omega = lax.all_gather(samples, ("row", "col"), axis=0, tiled=True)
+    size = lax.axis_size(("row", "col"))
+    parts = jnp.stack([samples for _ in range(size)])
+    parts = lax.all_to_all(parts, ("row", "col"), split_axis=0, concat_axis=0)
+    omega = jnp.concatenate(parts, axis=0)
     full = omega.shape[0]
     own = lax.dynamic_slice_in_dim(omega, lax.axis_index("col") * col_width, col_width, 0)
     direct = summed_on_arrival(jnp.dot(slab, own, preferred_element_type=jnp.float32), "col", 0)

time: 332 us -> 288 us (0.87)
  waiting for transfers between devices: 191 us -> 147 us
  between operations: 16.2 us -> 2.87 us
  starting transfers between devices: 23.8 us -> 36.8 us
  local copies, waits for them, and re-layouts: 25.6 us -> 29.1 us
    all_gather x1 -> x0, waiting for transfers between devices: 90.9 us -> none  [on_device(): omega = lax.all_gather(samples, ('row', 'col'), axis=0, tiled=True)]
    all_to_all x0 -> x1, waiting for transfers between devices: none -> 50.8 us  [on_device(): parts = lax.all_to_all(parts, ('row', 'col'), split_axis=0, concat_axis=0)]
    all_to_all x0 -> x1, starting transfers between devices: none -> 8.78 us  [on_device(): parts = lax.all_to_all(parts, ('row', 'col'), split_axis=0, concat_axis=0)]
    all_to_all x2, starting transfers between devices: 12.4 us -> 16.1 us  [summed_on_arrival(): pieces = lax.all_to_all(in_blocks(x, dim, devices), axis, 0, 0, tiled=True)]
    another operation x6 -> x7, local copies, waits for them, and re-layouts: 5.27 us -> 8.73 us
    all_to_all x1, waiting for transfers between devices: 47.6 us -> 44.2 us  [in_one_piece(): lax.all_to_all(both, axis, split_axis=split_dim, concat_axis=concat_dim,...]
  transfers between devices with their start and end apart: 5 -> 5, of which waited for: 4 -> 4; matrix products, arithmetic and copies ran while one was open for 7% -> 6% of each run, Pallas kernels for 0% -> 0%
where the time goes in v1:
time: 288 us; the launch traced here: 287 us
  waiting for transfers between devices  147 us (51%)
  other arithmetic  60.1 us (21%)
  starting transfers between devices  36.8 us (13%)
  local copies, waits for them, and re-layouts  29.1 us (10%)
  matrix products  11.1 us (4%)
    all_to_all x1, waiting for transfers between devices, on_device(): parts = lax.all_to_all(parts, ('row', 'col'), split_axis=0, concat_axis=0)  50.8 us
    all_to_all x1, waiting for transfers between devices, in_one_piece(): lax.all_to_all(both, axis, split_axis=split_dim, concat_axis=concat_dim,...  44.2 us
    another operation x6, other arithmetic, on_device(): lower = jnp.linalg.cholesky(gram)  34 us
    all_to_all x1, waiting for transfers between devices, sent_to_all(): return lax.all_to_all(copies, axis, split_axis=0, concat_axis=0, tiled=True)  26.1 us
    all_to_all x2, waiting for transfers between devices, summed_on_arrival(): pieces = lax.all_to_all(in_blocks(x, dim, devices), axis, 0, 0, tiled=True)  25.7 us
    another operation x3, other arithmetic, on_device(): lax.linalg.triangular_solve(lower, masked, left_side=False, lower=True, t...  20.5 us
    all_to_all x2, starting transfers between devices, summed_on_arrival(): pieces = lax.all_to_all(in_blocks(x, dim, devices), axis, 0, 0, tiled=True)  16.1 us
    all_to_all x1, starting transfers between devices, on_device(): parts = lax.all_to_all(parts, ('row', 'col'), split_axis=0, concat_axis=0)  8.78 us
  transfers between devices with their start and end apart: 5, of which 4 were waited for; matrix products, arithmetic and copies ran while one was open for 6% of the time, Pallas kernels for 0%

profile of v1, /device:TPU:1, one launch (start us, length us, event | category | flops | bytes accessed | tf_op | source)
XLA Modules:
  0.0 286.9 jit_solution(10269464225098588261)
XLA Ops:
  0.6 3.4 %stack.2 = bf16[32,256,256]{2,1,0:T(8,128)(2,1)} broadcast(bf16[256,256]{1,0:T(8,128)(2,1)} %param.8), dimensions={1,2} | broadcast | bytes 4325376 | tf_op jit(solution)/shard_map/stack | solution.py:44
  4.1 8.8 %all-to-all-start = ((bf16[32,256,256]{2,1,0:T(8,128)(2,1)}), bf16[32,256,256]{2,1,0:T(8,128)(2,1)}, u32[]{:S(2)}, u32[]{:S(2)}) async-start(bf16[32,256,256]{2,1,0:T(8,128)(2,1)} %stack.2), calls=%async_computation | async-start | bytes 8388608 | tf_op jit(solution)/shard_map/all_to_all | solution.py:45
  13.0 0.2 select_reduce_fusion.2
  13.2 0.2 fusion.2
  13.6 50.8 %all-to-all-done = bf16[32,256,256]{2,1,0:T(8,128)(2,1)} async-done(((bf16[32,256,256]{2,1,0:T(8,128)(2,1)}), bf16[32,256,256]{2,1,0:T(8,128)(2,1)}, u32[]{:S(2)}, u32[]{:S(2)}) %all-to-all-start) | async-done | bytes 4194336 | tf_op jit(solution)/shard_map/all_to_all | solution.py:45
  64.4 2.9 gather_fusion
  67.3 2.1 convolution_bitcast_fusion.1
  69.5 0.2 copy.27
  69.6 1.2 fusion.20
  70.8 2.5 copy.28
  73.3 2.7 reshape_reshape.17
  76.0 2.3 pad_maximum_fusion
  78.3 8.2 %all-to-all-start.2 = ((f32[8,2,32769]{2,1,0:T(2,128)}), f32[8,2,32769]{2,1,0:T(2,128)S(1)}, u32[]{:S(2)}, u32[]{:S(2)}) async-start(f32[8,2,32769]{2,1,0:T(2,128)} %pad_maximum_fusion), calls=%async_computation.2 | async-start | bytes 4210688 | tf_op jit(solution)/shard_map/all_to_all | solution.py:24
  86.5 2.3 convolution_bitcast_fusion
  88.9 2.0 copy.24
  90.9 44.2 %all-to-all-done.2 = f32[8,2,32769]{2,1,0:T(2,128)S(1)} async-done(((f32[8,2,32769]{2,1,0:T(2,128)}), f32[8,2,32769]{2,1,0:T(2,128)S(1)}, u32[]{:S(2)}, u32[]{:S(2)}) %all-to-all-start.2) | async-done | bytes 2097248 | tf_op jit(solution)/shard_map/all_to_all | solution.py:24
  135.1 5.1 %all-to-all-start.1 = ((f32[8,64,256]{2,1,0:T(8,128)}), f32[8,64,256]{2,1,0:T(8,128)}, u32[]{:S(2)}, u32[]{:S(2)}) async-start(f32[8,64,256]{2,1,0:T(8,128)} %bitcast.87), calls=%async_computation.1 | async-start | bytes 1048576 | tf_op jit(solution)/shard_map/all_to_all | solution.py:15
  140.1 1.5 split.9
  141.6 4.0 %reshape_reshape.19 = f32[16,128,256]{2,1,0:T(8,128)} reshape(f32[8,2,32768]{2,1,0:T(2,128)} %split.9) | data formatting | bytes 4194304 | tf_op jit(solution)/shard_map/reshape;reshape | solution.py:77
  145.7 0.2 fusion.16
  145.9 3.8 %fusion = f32[16,128,256]{2,0,1:T(8,128)S(1)} fusion(f32[16,128,256]{2,1,0:T(8,128)} %reshape_reshape.19, s32[16]{0:T(128)S(1)} %convert_element_type.32), kind=kOutput, calls=%fused_computation.4 | convolution fusion | flops 100663552 | bytes 4194368 | tf_op jit(solution)/shard_map/qj,qrs->jrs/dot_general | solution.py:78
  149.7 2.6 copy.31
  152.3 11.1 %all-to-all-start.3 = ((f32[32,64,256]{2,1,0:T(8,128)}), f32[32,64,256]{2,1,0:T(8,128)S(1)}, u32[]{:S(2)}, u32[]{:S(2)}) async-start(f32[32,64,256]{2,1,0:T(8,128)} %bitcast.16), calls=%async_computation.3 | async-start | bytes 4194304 | tf_op jit(solution)/shard_map/all_to_all | solution.py:15
  164.0 1.1 reduce_sum.40
  165.1 25.7 %all-to-all-done.3 = f32[32,64,256]{2,1,0:T(8,128)S(1)} async-done(((f32[32,64,256]{2,1,0:T(8,128)}), f32[32,64,256]{2,1,0:T(8,128)S(1)}, u32[]{:S(2)}, u32[]{:S(2)}) %all-to-all-start.3) | async-done | bytes 2097184 | tf_op jit(solution)/shard_map/all_to_all | solution.py:15
  190.9 0.6 broadcast_multiply_fusion
  191.6 0.4 fusion.31
  192.0 1.5 broadcast_in_dim.39
  193.5 3.8 %all-to-all-start.4 = ((f32[8,256,256]{2,1,0:T(8,128)}), f32[8,256,256]{2,1,0:T(8,128)S(1)}, u32[]{:S(2)}, u32[]{:S(2)}) async-start(f32[8,256,256]{2,1,0:T(8,128)} %broadcast_in_dim.39), calls=%async_computation.4 | async-start | bytes 4194304 | tf_op jit(solution)/shard_map/all_to_all | solution.py:31
  197.3 26.1 %all-to-all-done.4 = f32[8,256,256]{2,1,0:T(8,128)S(1)} async-done(((f32[8,256,256]{2,1,0:T(8,128)}), f32[8,256,256]{2,1,0:T(8,128)S(1)}, u32[]{:S(2)}, u32[]{:S(2)}) %all-to-all-start.4) | async-done | bytes 2097184 | tf_op jit(solution)/shard_map/all_to_all | solution.py:31
  223.4 0.1 reduce_sum.44
  223.6 0.1 copy.32
  223.8 11.7 %cholesky.49 = f32[128,128]{1,0:T(8,128)S(1)} custom-call(f32[128,128]{1,0:T(8,128)S(1)} %cholesky.115), custom_call_target="Cholesky" | custom-call | tf_op jit(solution)/shard_map/jit(cholesky)/cholesky | solution.py:86
  235.6 9.8 %custom-call.14 = f32[1,128,128]{1,2,0:T(8,128)S(1)} custom-call(f32[1,128,128]{2,1,0:T(8,128)S(1)} %get-tuple-element.25), custom_call_target="InvertDiagBlocksLowerTriangular" | custom-call | tf_op jit(solution)/shard_map/jit(cholesky)/cholesky | solution.py:86
  245.4 0.2 constant_dynamic-update-slice_fusion.1
  245.6 0.3 convolution_subtract_fusion
  245.9 11.7 %cholesky.103 = f32[128,128]{1,0:T(8,128)S(1)} custom-call(f32[128,128]{1,0:T(8,128)S(1)} %convolution_subtract_fusion), custom_call_target="Cholesky" | custom-call | tf_op jit(solution)/shard_map/jit(cholesky)/cholesky | solution.py:86
  257.7 0.7 compare_reduce_fusion
  259.8 5.3 %while.1 = (s32[]{:T(128)}, f32[256,256]{1,0:T(8,128)S(1)}, s32[2,2]{1,0:T(2,128)S(1)}, f32[2,128,128]{2,1,0:T(8,128)}, s32[]{:T(128)}) while((s32[]{:T(128)}, f32[256,256]{1,0:T(8,128)S(1)}, s32[2,2]{1,0:T(2,128)S(1)}, f32[2,128,128]{2,1,0:T(8,128)}, s32[]{:T(128)}) %tuple.28), condition=%wide.while_cond, body=%wide.while_body.sunk | while | flops 2 | bytes 132205 | solution.py:87
  259.9 0.6 fusion.42
  260.4 2.0 bitcast_dynamic-update-slice_fusion.2
  262.5 0.6 fusion.42
  263.1 2.0 bitcast_dynamic-update-slice_fusion.2
  265.1 20.5 %custom-call.15 = f32[2,128,128]{1,2,0:T(8,128)S(1)} custom-call(f32[2,128,128]{2,1,0:T(8,128)} %get-tuple-element.9), custom_call_target="InvertDiagBlocksLowerTriangular" | custom-call | tf_op jit(solution)/shard_map/triangular_solve | solution.py:87
  285.6 0.2 fusion.11
  285.8 0.2 convolution_subtract_fusion.1
  286.1 0.2 fusion.9
  286.3 0.6 maximum_bitcast_fusion
  (31 shorter events, 0.9 us)
Async XLA Ops:
  0.6 85.9 %copy-start = (bf16[1,512,1024]{2,1,0:T(8,128)(2,1)S(1)}, bf16[1,512,1024]{2,1,0:T(8,128)(2,1)}, u32[]{:S(2)}) copy-start(bf16[1,512,1024]{2,1,0:T(8,128)(2,1)} %param.7) | copy-start | bytes 3145732
  4.1 8.8 %copy-start.2 = (s32[2,1]{0,1:T(1,128)S(1)}, s32[2,1]{0,1:T(1,128)}, u32[]{:S(2)}) copy-start(s32[2,1]{0,1:T(1,128)} %param.10) | copy-start | bytes 28
  4.1 9.1 %copy-start.3 = (s32[2]{0:T(128)S(1)}, s32[2]{0:T(128)}, u32[]{:S(2)}) copy-start(s32[2]{0:T(128)} %param.11) | copy-start | bytes 28
  4.1 9.4 %copy-start.1 = (s32[2,16]{1,0:T(2,128)S(1)}, s32[2,16]{1,0:T(2,128)}, u32[]{:S(2)}) copy-start(s32[2,16]{1,0:T(2,128)} %param.12) | copy-start | bytes 388
  4.1 60.4 %all-to-all-start = ((bf16[32,256,256]{2,1,0:T(8,128)(2,1)}), bf16[32,256,256]{2,1,0:T(8,128)(2,1)}, u32[]{:S(2)}, u32[]{:S(2)}) async-start(bf16[32,256,256]{2,1,0:T(8,128)(2,1)} %stack.2), calls=%async_computation | async-start | bytes 8388608 | tf_op jit(solution)/shard_map/all_to_all | solution.py:45
  78.3 56.7 %all-to-all-start.2 = ((f32[8,2,32769]{2,1,0:T(2,128)}), f32[8,2,32769]{2,1,0:T(2,128)S(1)}, u32[]{:S(2)}, u32[]{:S(2)}) async-start(f32[8,2,32769]{2,1,0:T(2,128)} %pad_maximum_fusion), calls=%async_computation.2 | async-start | bytes 4210688 | tf_op jit(solution)/shard_map/all_to_all | solution.py:24
  135.1 17.2 %all-to-all-start.1 = ((f32[8,64,256]{2,1,0:T(8,128)}), f32[8,64,256]{2,1,0:T(8,128)}, u32[]{:S(2)}, u32[]{:S(2)}) async-start(f32[8,64,256]{2,1,0:T(8,128)} %bitcast.87), calls=%async_computation.1 | async-start | bytes 1048576 | tf_op jit(solution)/shard_map/all_to_all | solution.py:15
  152.3 38.5 %all-to-all-start.3 = ((f32[32,64,256]{2,1,0:T(8,128)}), f32[32,64,256]{2,1,0:T(8,128)S(1)}, u32[]{:S(2)}, u32[]{:S(2)}) async-start(f32[32,64,256]{2,1,0:T(8,128)} %bitcast.16), calls=%async_computation.3 | async-start | bytes 4194304 | tf_op jit(solution)/shard_map/all_to_all | solution.py:15
  193.5 29.9 %all-to-all-start.4 = ((f32[8,256,256]{2,1,0:T(8,128)}), f32[8,256,256]{2,1,0:T(8,128)S(1)}, u32[]{:S(2)}, u32[]{:S(2)}) async-start(f32[8,256,256]{2,1,0:T(8,128)} %broadcast_in_dim.39), calls=%async_computation.4 | async-start | bytes 4194304 | tf_op jit(solution)/shard_map/all_to_all | solution.py:31
